TPU v7x, 32 devices: a whole 2x2x4 slice. The times are simulated.
32 devices in a mesh: parts: 2 (over y), pencil: 4 (over z), slab: 2 (over x), field: 2 (over core).
Axes of the slice: x: 2, y: 2, z: 4, core: 2. Of those that a mesh axis runs over, the one named last changes fastest.
Arguments:
- state: bfloat16 [16, 2, 512, 512], P('parts', 'slab', 'pencil'), parts along dimension 0, may hold values from -6 to 6
- tangents: bfloat16 [16, 8, 2, 512, 512], P(('parts', 'field'), None, 'slab', 'pencil'), parts along dimension 0, may hold values from -6 to 6
- d1: bfloat16 [512, 512], replicated, may hold values from -0.25 to 0.25
- d2: bfloat16 [512, 512], replicated, may hold values from -0.25 to 0.25
- filt: bfloat16 [512, 512], replicated, may hold values from -0.25 to 0.25
- advect: float32 [2, 8], replicated, may hold values from 0.3 to 1
- diffuse: float32 [8], replicated, may hold values from 0.3 to 1
- coef: float32 [8, 8], replicated, may hold values from -3 to 3
- rates: float32 [8, 8], replicated, may hold values from -3.6 to 3.6
Outputs:
- state_out: bfloat16 [16, 2, 512, 512], P('parts', 'slab', 'pencil'), parts along dimension 0
- tangent_out: bfloat16 [16, 8, 2, 512, 512], P(('parts', 'field'), None, 'slab', 'pencil'), parts along dimension 0
There are 2 independent parts, one for each index of `parts`. A program takes and returns all parts, laid end to end along the dimension named above; an argument that names none is the same for every part. Nothing has to cross between parts.
All inputs are finite; a program needn't handle non-finite values.
Results may differ from a plain program's by a relative error of at most 0.0094.
Values may be sent and summed in bfloat16 or wider, within the bound.
No kernel may reach another device: no remote copies, remote signals or barrier semaphores. Data moves between devices by JAX's collectives and lax.ppermute only.
A program may use at most 128 MiB of HBM per device.

v0:
```python
import jax
import jax.numpy as jnp
from jax import lax
from jax.sharding import PartitionSpec as P

highest = lax.Precision.HIGHEST
time_step = 0.4


def spread(values, fields):
    return values.reshape(values.shape + (1,) * (fields.ndim - values.ndim))


def reaction(state, tangent, coef, rates, offset):
    state_float = state.astype(jnp.float32)
    argument = jnp.einsum("ps,s...->p...", rates, state_float, precision=highest)
    activity = jnp.tanh(argument)
    slopes = 1.0 - activity * activity
    state_rate = jnp.einsum("ps,p...->s...", coef, activity, precision=highest)
    tangent_float = tangent.astype(jnp.float32)
    mixing = jnp.einsum("pt,qt...->qp...", rates, tangent_float, precision=highest)
    number = tangent.shape[0]
    own_coef = lax.dynamic_slice_in_dim(coef, offset, number, 0)
    own_activity = lax.dynamic_slice_in_dim(activity, offset, number, 0)
    tangent_rate = jnp.einsum("ps,qp...->qs...", coef, slopes[None] * mixing, precision=highest)
    tangent_rate = tangent_rate + spread(own_coef, tangent) * own_activity[:, None]
    return (state_rate, tangent_rate)


def update(fields, rate, speeds, diffusivity, operators):
    derivative_op, diffusion_op, filter_op = operators
    slope_term = jnp.dot(fields, derivative_op, preferred_element_type=jnp.float32)
    curve_term = jnp.dot(fields, diffusion_op, preferred_element_type=jnp.float32)
    middle = fields.astype(jnp.float32) + time_step * (
        spread(diffusivity, fields) * curve_term - spread(speeds, fields) * slope_term + rate
    )
    middle = middle.astype(jnp.bfloat16)
    return jnp.dot(middle, filter_op, preferred_element_type=jnp.float32).astype(jnp.bfloat16)


def local(state, tangents, d1, d2, filt, advect, diffuse, coef, rates):
    field_index = lax.axis_index("field")
    params_here = tangents.shape[0]
    state_count = state.shape[0]
    offset = field_index * params_here
    operators = (d1, d2, filt)
    for direction in range(2):
        speeds = advect[direction]
        state_rate, tangent_rate = reaction(state, tangents, coef, rates, offset)
        tangents = update(tangents, tangent_rate, speeds[None, :], diffuse[None, :], operators)
        outgoing = update(state, state_rate, speeds, diffuse, operators)
        merged = tangents.reshape((params_here * state_count,) + tangents.shape[2:])
        arrived, merged = (
            lax.all_to_all(outgoing, "pencil", split_axis=3, concat_axis=2, tiled=True),
            lax.all_to_all(merged, "pencil", split_axis=3, concat_axis=2, tiled=True),
        )
        arrived = jnp.swapaxes(arrived, 2, 3)
        merged = jnp.swapaxes(merged, 2, 3)
        tangents = merged.reshape((params_here, state_count) + merged.shape[1:])
        state = arrived
    return (state, tangents)


def solution(mesh):
    in_specs = (
        P("parts", "slab", "pencil", None),
        P(("parts", "field"), None, "slab", "pencil", None),
        P(),
        P(),
        P(),
        P(),
        P(),
        P(),
        P(),
    )
    out_specs = (
        P("parts", "slab", "pencil", None),
        P(("parts", "field"), None, "slab", "pencil", None),
    )
    return jax.shard_map(local, mesh=mesh, in_specs=in_specs, out_specs=out_specs, check_vma=False)
```

profile of v0, /device:TPU:0, one launch (start us, length us, event | category | flops | bytes accessed | tf_op | source)
XLA Modules:
  0.0 366.4 jit_solution(3940533547604179620)
XLA Ops:
  1.7 3.2 fusion.76
  5.0 2.1 multiply_subtract_fusion
  8.4 3.3 fusion.83
  11.7 6.4 %fusion.54 = bf16[8,1,128,512]{3,2,0,1:T(8,128)(2,1)} fusion(f32[128,512,8]{1,2,0:T(8,128)} %fusion.83, f32[8,128,512]{2,1,0:T(8,128)} %fusion.76, bf16[8,1,128,512]{3,2,1,0:T(8,128)(2,1)} %param.9, f32[8]{0:T(128)S(1)} %get-tuple-element.7, f32[8]{0:T(128)S(1)} %copy-done.10, bf16[512,512]{1,0:T(8,128)(2,1)S(1)} %copy-done.9, bf16[512,512]{1,0:T(8,128)(2,1)} %param.11), kind=kOutput, calls=%fused_computation.58 | convolution fusion | flops 1078460416 | bytes 7340096 | tf_op jit(solution)/shard_map/dot_general | solution.py:38
  18.1 2.4 copy.82
  20.5 6.5 %all-to-all-start = ((bf16[8,1,128,512]{2,0,1,3:T(8,128)(2,1)}), bf16[8,1,128,512]{2,0,1,3:T(8,128)(2,1)}, u32[]{:S(2)}, u32[]{:S(2)}) async-start(bf16[8,1,128,512]{2,0,1,3:T(8,128)(2,1)} %copy.82), calls=%async_computation | async-start | bytes 2097152 | tf_op jit(solution)/shard_map/all_to_all | solution.py:54
  30.4 5.7 %fusion.66 = f32[4,8,128,512]{3,2,1,0:T(8,128)} fusion(bf16[512,512]{1,0:T(8,128)(2,1)S(1)} %copy-done, bf16[4,8,1,128,512]{4,3,2,1,0:T(8,128)(2,1)S(1)} %copy-done.2), kind=kOutput, calls=%fused_computation.70 | convolution fusion | flops 2147483648 | bytes 13107200 | tf_op jit(solution)/shard_map/dot_general | solution.py:33
  36.1 5.6 %fusion.21 = f32[4,128,512,8]{2,3,1,0:T(8,128)S(1)} fusion(bf16[4,8,128,512]{3,2,1,0:T(8,128)(2,1)S(1)} %bitcast.280, f32[8,8]{1,0:T(8,128)S(1)} %copy-done.8), kind=kOutput, calls=%fused_computation.22 | convolution fusion | flops 201326592 | bytes 12583168 | tf_op jit(solution)/shard_map/pt,qt...->qp.../dot_general | solution.py:21
  41.7 10.2 %fusion.12 = f32[4,128,512,8]{2,3,1,0:T(8,128)} fusion(f32[4,128,512,8]{2,3,1,0:T(8,128)S(1)} %fusion.21, f32[8,128,512]{2,0,1:T(8,128)S(1)} %get-tuple-element.8, f32[8,8]{1,0:T(8,128)S(1)} %copy-done.7), kind=kOutput, calls=%fused_computation.15 | convolution fusion | flops 203423744 | bytes 18874624 | tf_op jit(solution)/shard_map/ps,qp...->qs.../dot_general | solution.py:25
  51.9 20.5 %fusion.39 = bf16[4,8,128,512]{3,2,1,0:T(8,128)(2,1)} fusion(f32[4,128,512,8]{2,3,1,0:T(8,128)} %fusion.12, f32[4,8,128,512]{3,2,1,0:T(8,128)} %fusion.66, bf16[4,8,1,128,512]{4,3,2,1,0:T(8,128)(2,1)} %param.10, f32[4,128,512]{2,1,0:T(8,128)} %copy.93, f32[4,8]{1,0:T(4,128)S(1)} %constant_dynamic-slice_fusion.1, f32[8]{0:T(128)S(1)} %get-tuple-element.7, ...), kind=kOutput, calls=%fused_computation.37 | convolution fusion | flops 4318035968 | bytes 27263168 | tf_op jit(solution)/shard_map/dot_general | solution.py:38
  72.3 7.9 %copy.94 = bf16[32,1,128,512]{2,0,1,3:T(8,128)(2,1)} copy(bf16[32,1,128,512]{3,2,0,1:T(8,128)(2,1)} %bitcast.285) | data formatting | bytes 8388608 | tf_op jit(solution)/shard_map/reshape | solution.py:52
  80.3 5.4 %all-to-all-start.2 = ((bf16[32,1,128,512]{2,0,1,3:T(8,128)(2,1)}), bf16[32,1,128,512]{2,0,1,3:T(8,128)(2,1)}, u32[]{:S(2)}, u32[]{:S(2)}) async-start(bf16[32,1,128,512]{2,0,1,3:T(8,128)(2,1)} %copy.94), calls=%async_computation.2 | async-start | bytes 8388608 | tf_op jit(solution)/shard_map/all_to_all | solution.py:55
  85.6 2.0 copy.151
  90.2 2.7 fusion.49
  94.3 3.3 fusion.47
  97.6 6.4 %fusion.55 = bf16[8,1,128,512]{3,2,0,1:T(8,128)(2,1)} fusion(f32[128,512,8]{1,2,0:T(8,128)} %fusion.47, f32[8,128,512]{2,1,0:T(8,128)} %fusion.74, bf16[8,1,512,128]{2,3,0,1:T(8,128)(2,1)} %copy-done.5, f32[8]{0:T(128)S(1)} %get-tuple-element.6, f32[8]{0:T(128)S(1)} %copy-done.10, bf16[512,512]{1,0:T(8,128)(2,1)S(1)} %copy-done.9, bf16[512,512]{1,0:T(8,128)(2,1)} %param.11), kind=kOutput, calls=%fused_computation.59 | convolution fusion | flops 1078460416 | bytes 7340096 | tf_op jit(solution)/shard_map/dot_general | solution.py:38
  104.0 2.4 copy.87
  109.6 69.0 %all-to-all-done.2 = bf16[32,1,128,512]{2,0,1,3:T(8,128)(2,1)} async-done(((bf16[32,1,128,512]{2,0,1,3:T(8,128)(2,1)}), bf16[32,1,128,512]{2,0,1,3:T(8,128)(2,1)}, u32[]{:S(2)}, u32[]{:S(2)}) %all-to-all-start.2) | async-done | bytes 4194336 | tf_op jit(solution)/shard_map/all_to_all | solution.py:55
  178.6 4.7 %all-to-all-start.1 = ((bf16[8,1,128,512]{2,0,1,3:T(8,128)(2,1)}), bf16[8,1,128,512]{2,0,1,3:T(8,128)(2,1)}, u32[]{:S(2)}, u32[]{:S(2)}) async-start(bf16[8,1,128,512]{2,0,1,3:T(8,128)(2,1)} %copy.87), calls=%async_computation.1 | async-start | bytes 2097152 | tf_op jit(solution)/shard_map/all_to_all | solution.py:54
  183.3 7.4 %copy.95 = bf16[32,1,4,128,128]{3,2,4,0,1:T(4,128)(2,1)} copy(bf16[32,1,4,128,128]{3,0,4,2,1:T(8,128)(2,1)} %bitcast.47) | data formatting | bytes 8388608 | tf_op jit(solution)/shard_map/all_to_all | solution.py:55
  190.7 7.2 %all_to_all.63 = bf16[32,1,512,128]{2,3,0,1:T(8,128)(2,1)} reshape(bf16[32,1,4,128,128]{3,2,4,0,1:T(4,128)(2,1)} %copy.95) | data formatting | bytes 8388608 | tf_op jit(solution)/shard_map/all_to_all | solution.py:55
  197.9 8.0 %fusion.19 = f32[4,128,512,8]{2,3,1,0:T(8,128)S(1)} fusion(bf16[4,8,128,512]{3,2,1,0:T(8,128)(2,1)} %bitcast.276, f32[8,8]{1,0:T(8,128)S(1)} %copy-done.8), kind=kOutput, calls=%fused_computation.20 | convolution fusion | flops 201326592 | bytes 12583168 | tf_op jit(solution)/shard_map/pt,qt...->qp.../dot_general | solution.py:21
  205.9 5.6 %fusion.64 = f32[4,8,128,512]{3,2,1,0:T(8,128)} fusion(bf16[4,8,128,512]{3,2,1,0:T(8,128)(2,1)S(1)} %bitcast.279, bf16[512,512]{1,0:T(8,128)(2,1)S(1)} %copy-done), kind=kOutput, calls=%fused_computation.68 | convolution fusion | flops 2147483648 | bytes 13107200 | tf_op jit(solution)/shard_map/dot_general | solution.py:33
  211.5 10.1 %fusion.5 = f32[4,128,512,8]{2,3,1,0:T(8,128)} fusion(f32[4,128,512,8]{2,3,1,0:T(8,128)S(1)} %fusion.19, f32[8,128,512]{2,0,1:T(8,128)S(1)} %get-tuple-element.10, f32[8,8]{1,0:T(8,128)S(1)} %copy-done.7), kind=kOutput, calls=%fused_computation.7 | convolution fusion | flops 203423744 | bytes 18874624 | tf_op jit(solution)/shard_map/ps,qp...->qs.../dot_general | solution.py:25
  221.6 20.4 %fusion.42 = bf16[4,8,128,512]{3,2,1,0:T(8,128)(2,1)} fusion(f32[4,128,512]{2,1,0:T(8,128)} %copy.99, f32[4,128,512,8]{2,3,1,0:T(8,128)} %fusion.5, f32[4,8,128,512]{3,2,1,0:T(8,128)} %fusion.64, bf16[4,8,1,128,512]{4,3,1,0,2:T(8,128)(2,1)} %bitcast.278, f32[8]{0:T(128)S(1)} %get-tuple-element.6, f32[4,8]{1,0:T(4,128)S(1)} %constant_dynamic-slice_fusion.1, ...), kind=kOutput, calls=%fused_computation.38 | convolution fusion | flops 4318035968 | bytes 31457472 | tf_op jit(solution)/shard_map/dot_general | solution.py:38
  242.0 7.9 %copy.100 = bf16[32,1,128,512]{2,0,1,3:T(8,128)(2,1)} copy(bf16[32,1,128,512]{3,2,0,1:T(8,128)(2,1)} %bitcast.284) | data formatting | bytes 8388608 | tf_op jit(solution)/shard_map/reshape | solution.py:52
  249.9 5.3 %all-to-all-start.3 = ((bf16[32,1,128,512]{2,0,1,3:T(8,128)(2,1)}), bf16[32,1,128,512]{2,0,1,3:T(8,128)(2,1)}, u32[]{:S(2)}, u32[]{:S(2)}) async-start(bf16[32,1,128,512]{2,0,1,3:T(8,128)(2,1)} %copy.100), calls=%async_computation.3 | async-start | bytes 8388608 | tf_op jit(solution)/shard_map/all_to_all | solution.py:55
  255.2 2.0 copy.88
  258.4 89.3 %all-to-all-done.3 = bf16[32,1,128,512]{2,0,1,3:T(8,128)(2,1)} async-done(((bf16[32,1,128,512]{2,0,1,3:T(8,128)(2,1)}), bf16[32,1,128,512]{2,0,1,3:T(8,128)(2,1)}, u32[]{:S(2)}, u32[]{:S(2)}) %all-to-all-start.3) | async-done | bytes 4194336 | tf_op jit(solution)/shard_map/all_to_all | solution.py:55
  347.7 5.8 %copy.101 = bf16[32,1,128,512]{2,3,0,1:T(8,128)(2,1)} copy(bf16[32,1,128,512]{2,0,1,3:T(8,128)(2,1)} %all-to-all-done.3) | data formatting | bytes 8388608 | tf_op jit(solution)/shard_map/all_to_all | solution.py:55
  353.6 6.5 %copy.102 = bf16[32,1,4,128,128]{4,3,2,0,1:T(8,128)(2,1)} copy(bf16[32,1,4,128,128]{3,4,2,0,1:T(8,128)(2,1)} %bitcast.281) | data formatting | bytes 8388608 | tf_op jit(solution)/shard_map/all_to_all | solution.py:55
  360.0 6.2 %copy.103 = bf16[4,8,1,128,512]{4,3,2,1,0:T(8,128)(2,1)} copy(bf16[4,8,1,128,512]{3,4,1,0,2:T(8,128)(2,1)} %bitcast.282) | data formatting | bytes 8388608
  (33 shorter events, 14.0 us)
Async XLA Ops:
  0.6 1.1 copy-start
  0.6 4.3 %copy-start.6 = (bf16[8,1,128,512]{3,2,1,0:T(8,128)(2,1)S(1)}, bf16[8,1,128,512]{3,2,1,0:T(8,128)(2,1)}, u32[]{:S(2)}) copy-start(bf16[8,1,128,512]{3,2,1,0:T(8,128)(2,1)} %param.9) | copy-start | bytes 3145732
  1.7 6.7 %copy-start.7 = (f32[8,8]{1,0:T(8,128)S(1)}, f32[8,8]{1,0:T(8,128)}, u32[]{:S(2)}) copy-start(f32[8,8]{1,0:T(8,128)} %param.16) | copy-start | bytes 772
  5.0 6.7 %copy-start.9 = (bf16[512,512]{1,0:T(8,128)(2,1)S(1)}, bf16[512,512]{1,0:T(8,128)(2,1)}, u32[]{:S(2)}) copy-start(bf16[512,512]{1,0:T(8,128)(2,1)} %param.13) | copy-start | bytes 1572868
  5.0 6.7 %copy-start.10 = (f32[8]{0:T(128)S(1)}, f32[8]{0:T(128)}, u32[]{:S(2)}) copy-start(f32[8]{0:T(128)} %param.15) | copy-start | bytes 100
  7.1 1.3 copy-start.3
  20.5 59.7 %all-to-all-start = ((bf16[8,1,128,512]{2,0,1,3:T(8,128)(2,1)}), bf16[8,1,128,512]{2,0,1,3:T(8,128)(2,1)}, u32[]{:S(2)}, u32[]{:S(2)}) async-start(bf16[8,1,128,512]{2,0,1,3:T(8,128)(2,1)} %copy.82), calls=%async_computation | async-start | bytes 2097152 | tf_op jit(solution)/shard_map/all_to_all | solution.py:54
  27.1 3.3 copy-start.2
  30.4 5.7 %copy-start.8 = (f32[8,8]{1,0:T(8,128)S(1)}, f32[8,8]{1,0:T(8,128)}, u32[]{:S(2)}) copy-start(f32[8,8]{1,0:T(8,128)} %param.17) | copy-start | bytes 772
  80.3 98.3 %all-to-all-start.2 = ((bf16[32,1,128,512]{2,0,1,3:T(8,128)(2,1)}), bf16[32,1,128,512]{2,0,1,3:T(8,128)(2,1)}, u32[]{:S(2)}, u32[]{:S(2)}) async-start(bf16[32,1,128,512]{2,0,1,3:T(8,128)(2,1)} %copy.94), calls=%async_computation.2 | async-start | bytes 8388608 | tf_op jit(solution)/shard_map/all_to_all | solution.py:55
  88.1 2.0 copy-start.5
  92.9 1.4 copy-start.4
  178.6 71.3 %all-to-all-start.1 = ((bf16[8,1,128,512]{2,0,1,3:T(8,128)(2,1)}), bf16[8,1,128,512]{2,0,1,3:T(8,128)(2,1)}, u32[]{:S(2)}, u32[]{:S(2)}) async-start(bf16[8,1,128,512]{2,0,1,3:T(8,128)(2,1)} %copy.87), calls=%async_computation.1 | async-start | bytes 2097152 | tf_op jit(solution)/shard_map/all_to_all | solution.py:54
  197.9 8.0 %copy-start.1 = (bf16[32,1,512,128]{2,3,0,1:T(8,128)(2,1)S(1)}, bf16[32,1,512,128]{2,3,0,1:T(8,128)(2,1)}, u32[]{:S(2)}) copy-start(bf16[32,1,512,128]{2,3,0,1:T(8,128)(2,1)} %all_to_all.63) | copy-start | bytes 12582916
  249.9 97.8 %all-to-all-start.3 = ((bf16[32,1,128,512]{2,0,1,3:T(8,128)(2,1)}), bf16[32,1,128,512]{2,0,1,3:T(8,128)(2,1)}, u32[]{:S(2)}, u32[]{:S(2)}) async-start(bf16[32,1,128,512]{2,0,1,3:T(8,128)(2,1)} %copy.100), calls=%async_computation.3 | async-start | bytes 8388608 | tf_op jit(solution)/shard_map/all_to_all | solution.py:55
where the time goes:
time: 373 us; the launch traced here: 366 us
  waiting for transfers between devices  158 us (42%)
  matrix products  115 us (31%)
  local copies, waits for them, and re-layouts  69.8 us (19%)
  starting transfers between devices  21.9 us (6%)
    all_to_all x2, waiting for transfers between devices, local(): lax.all_to_all(merged, 'pencil', split_axis=3, concat_axis=2, tiled=True)  158 us
    dot_general x4, matrix products, update(): jnp.dot(middle, filter_op, preferred_element_type=jnp.float32)  53.6 us
    all_to_all x4, local copies, waits for them, and re-layouts, local(): lax.all_to_all(merged, 'pencil', split_axis=3, concat_axis=2, tiled=True)  26.9 us
    dot_general x2, matrix products, reaction(): jnp.einsum('ps,qp...->qs...', coef, slopes[None] * mixing, precision=high...  20.3 us
    dot_general x4, matrix products, update(): jnp.dot(fields, diffusion_op, preferred_element_type=jnp.float32)  16.5 us
    reshape x2, local copies, waits for them, and re-layouts, local(): merged = tangents.reshape((params_here * state_count,) + tangents.shape[2:])  15.8 us
    dot_general x2, matrix products, reaction(): jnp.einsum('pt,qt...->qp...', rates, tangent_float, precision=highest)  13.6 us
    all_to_all x2, starting transfers between devices, local(): lax.all_to_all(outgoing, 'pencil', split_axis=3, concat_axis=2, tiled=True)  11.2 us
  transfers between devices with their start and end apart: 4, of which 2 were waited for; matrix products, arithmetic and copies ran while one was open for 37% of the time, Pallas kernels for 0%

commit v1 on v0

--- a/solution.py
+++ b/solution.py
@@ -5,6 +5,13 @@
 
 highest = lax.Precision.HIGHEST
 time_step = 0.4
+
+
+def swap_blocks(x, axis, split, join):
+    peers = lax.axis_size(axis)
+    parts = jnp.stack(jnp.split(x, peers, axis=split), axis=0)
+    parts = lax.all_to_all(parts, axis, split_axis=0, concat_axis=0)
+    return jnp.concatenate(parts, axis=join)
 
 
 def spread(values, fields):
@@ -52,7 +59,7 @@
         merged = tangents.reshape((params_here * state_count,) + tangents.shape[2:])
         arrived, merged = (
             lax.all_to_all(outgoing, "pencil", split_axis=3, concat_axis=2, tiled=True),
-            lax.all_to_all(merged, "pencil", split_axis=3, concat_axis=2, tiled=True),
+            swap_blocks(merged, "pencil", 3, 2),
         )
         arrived = jnp.swapaxes(arrived, 2, 3)
         merged = jnp.swapaxes(merged, 2, 3)

time: 373 us -> 360 us (0.965)
  local copies, waits for them, and re-layouts: 69.8 us -> 52 us
  other arithmetic: 0 us -> 4.59 us
    all_to_all x4 -> x1, local copies, waits for them, and re-layouts: 26.9 us -> 4.78 us  [swap_blocks(): parts = lax.all_to_all(parts, axis, split_axis=0, concat_axis=0)]
    another operation x4 -> x6, local copies, waits for them, and re-layouts: 6.44 us -> 12 us
    another operation x0 -> x2, other arithmetic: none -> 4.59 us  [swap_blocks(): parts = jnp.stack(jnp.split(x, peers, axis=split), axis=0)]
  transfers between devices with their start and end apart: 4 -> 4, of which waited for: 2 -> 2; matrix products, arithmetic and copies ran while one was open for 37% -> 39% of each run, Pallas kernels for 0% -> 0%
where the time goes in v1:
time: 360 us; the launch traced here: 354 us
  waiting for transfers between devices  158 us (44%)
  matrix products  116 us (32%)
  local copies, waits for them, and re-layouts  52 us (14%)
  starting transfers between devices  21.8 us (6%)
  other arithmetic  4.59 us (1%)
    all_to_all x2, waiting for transfers between devices, swap_blocks(): parts = lax.all_to_all(parts, axis, split_axis=0, concat_axis=0)  158 us
    dot_general x4, matrix products, update(): jnp.dot(middle, filter_op, preferred_element_type=jnp.float32)  54 us
    dot_general x2, matrix products, reaction(): jnp.einsum('ps,qp...->qs...', coef, slopes[None] * mixing, precision=high...  20.1 us
    dot_general x4, matrix products, update(): jnp.dot(fields, diffusion_op, preferred_element_type=jnp.float32)  16.5 us
    reshape x2, local copies, waits for them, and re-layouts, swap_blocks(): return jnp.concatenate(parts, axis=join)  14.6 us
    dot_general x2, matrix products, reaction(): jnp.einsum('pt,qt...->qp...', rates, tangent_float, precision=highest)  13.6 us
    all_to_all x2, starting transfers between devices, local(): lax.all_to_all(outgoing, 'pencil', split_axis=3, concat_axis=2, tiled=True)  11.4 us
    all_to_all x2, starting transfers between devices, swap_blocks(): parts = lax.all_to_all(parts, axis, split_axis=0, concat_axis=0)  10.4 us
  transfers between devices with their start and end apart: 4, of which 2 were waited for; matrix products, arithmetic and copies ran while one was open for 39% of the time, Pallas kernels for 0%

profile of v1, /device:TPU:0, one launch (start us, length us, event | category | flops | bytes accessed | tf_op | source)
XLA Modules:
  0.0 353.7 jit_solution(4262573621626134658)
XLA Ops:
  1.7 3.2 fusion.76
  5.0 2.1 multiply_subtract_fusion
  8.4 3.3 fusion.83
  11.7 6.4 %fusion.54 = bf16[8,1,128,512]{3,2,0,1:T(8,128)(2,1)} fusion(f32[128,512,8]{1,2,0:T(8,128)} %fusion.83, f32[8,128,512]{2,1,0:T(8,128)} %fusion.76, bf16[8,1,128,512]{3,2,1,0:T(8,128)(2,1)} %param.9, f32[8]{0:T(128)S(1)} %get-tuple-element.15, f32[8]{0:T(128)S(1)} %copy-done.10, bf16[512,512]{1,0:T(8,128)(2,1)S(1)} %copy-done.9, bf16[512,512]{1,0:T(8,128)(2,1)} %param.11), kind=kOutput, calls=%fused_computation.60 | convolution fusion | flops 1078460416 | bytes 7340096 | tf_op jit(solution)/shard_map/dot_general | solution.py:45
  18.1 2.4 copy.57
  20.5 6.9 %all-to-all-start = ((bf16[8,1,128,512]{2,0,1,3:T(8,128)(2,1)}), bf16[8,1,128,512]{2,0,1,3:T(8,128)(2,1)}, u32[]{:S(2)}, u32[]{:S(2)}) async-start(bf16[8,1,128,512]{2,0,1,3:T(8,128)(2,1)} %copy.57), calls=%async_computation | async-start | bytes 2097152 | tf_op jit(solution)/shard_map/all_to_all | solution.py:61
  30.7 5.7 %fusion.66 = f32[4,8,128,512]{3,2,1,0:T(8,128)} fusion(bf16[512,512]{1,0:T(8,128)(2,1)S(1)} %copy-done, bf16[4,8,1,128,512]{4,3,2,1,0:T(8,128)(2,1)S(1)} %copy-done.2), kind=kOutput, calls=%fused_computation.80 | convolution fusion | flops 2147483648 | bytes 13107200 | tf_op jit(solution)/shard_map/dot_general | solution.py:40
  36.4 5.6 %fusion.21 = f32[4,128,512,8]{2,3,1,0:T(8,128)S(1)} fusion(bf16[4,8,128,512]{3,2,1,0:T(8,128)(2,1)S(1)} %bitcast.293, f32[8,8]{1,0:T(8,128)S(1)} %copy-done.8), kind=kOutput, calls=%fused_computation.24 | convolution fusion | flops 201326592 | bytes 12583168 | tf_op jit(solution)/shard_map/pt,qt...->qp.../dot_general | solution.py:28
  42.0 10.2 %fusion.12 = f32[4,128,512,8]{2,3,1,0:T(8,128)} fusion(f32[4,128,512,8]{2,3,1,0:T(8,128)S(1)} %fusion.21, f32[8,128,512]{2,0,1:T(8,128)S(1)} %get-tuple-element.16, f32[8,8]{1,0:T(8,128)S(1)} %copy-done.7), kind=kOutput, calls=%fused_computation.15 | convolution fusion | flops 203423744 | bytes 18874624 | tf_op jit(solution)/shard_map/ps,qp...->qs.../dot_general | solution.py:32
  52.2 20.5 %fusion.39 = bf16[4,8,128,512]{3,2,1,0:T(8,128)(2,1)} fusion(f32[4,128,512,8]{2,3,1,0:T(8,128)} %fusion.12, f32[4,8,128,512]{3,2,1,0:T(8,128)} %fusion.66, bf16[4,8,1,128,512]{4,3,2,1,0:T(8,128)(2,1)} %param.10, f32[4,128,512]{2,1,0:T(8,128)} %copy.68, f32[4,8]{1,0:T(4,128)S(1)} %constant_dynamic-slice_fusion.1, f32[8]{0:T(128)S(1)} %get-tuple-element.15, ...), kind=kOutput, calls=%fused_computation.39 | convolution fusion | flops 4318035968 | bytes 27263168 | tf_op jit(solution)/shard_map/dot_general | solution.py:45
  72.6 2.8 slice_bitcast_fusion.7
  75.4 2.3 pad_maximum_fusion
  77.7 5.3 %all-to-all-start.2 = ((bf16[4,32,1,128,128]{4,3,1,2,0:T(8,128)(2,1)}), bf16[4,32,1,128,128]{4,3,1,2,0:T(8,128)(2,1)}, u32[]{:S(2)}, u32[]{:S(2)}) async-start(bf16[4,32,1,128,128]{4,3,1,2,0:T(8,128)(2,1)} %pad_maximum_fusion), calls=%async_computation.2 | async-start | bytes 8388608 | tf_op jit(solution)/shard_map/all_to_all | solution.py:13
  85.5 2.1 fusion.74
  87.6 2.7 fusion.49
  91.7 3.3 fusion.47
  95.0 6.4 %fusion.55 = bf16[8,1,128,512]{3,2,0,1:T(8,128)(2,1)} fusion(f32[128,512,8]{1,2,0:T(8,128)} %fusion.47, f32[8,128,512]{2,1,0:T(8,128)} %fusion.74, bf16[8,1,512,128]{2,3,0,1:T(8,128)(2,1)} %copy-done.5, f32[8]{0:T(128)S(1)} %get-tuple-element.14, f32[8]{0:T(128)S(1)} %copy-done.10, bf16[512,512]{1,0:T(8,128)(2,1)S(1)} %copy-done.9, bf16[512,512]{1,0:T(8,128)(2,1)} %param.11), kind=kOutput, calls=%fused_computation.61 | convolution fusion | flops 1078460416 | bytes 7340096 | tf_op jit(solution)/shard_map/dot_general | solution.py:45
  101.4 2.4 copy.62
  107.0 69.0 %all-to-all-done.2 = bf16[4,32,1,128,128]{4,3,1,2,0:T(8,128)(2,1)} async-done(((bf16[4,32,1,128,128]{4,3,1,2,0:T(8,128)(2,1)}), bf16[4,32,1,128,128]{4,3,1,2,0:T(8,128)(2,1)}, u32[]{:S(2)}, u32[]{:S(2)}) %all-to-all-start.2) | async-done | bytes 4194336 | tf_op jit(solution)/shard_map/all_to_all | solution.py:13
  176.0 4.5 %all-to-all-start.1 = ((bf16[8,1,128,512]{2,0,1,3:T(8,128)(2,1)}), bf16[8,1,128,512]{2,0,1,3:T(8,128)(2,1)}, u32[]{:S(2)}, u32[]{:S(2)}) async-start(bf16[8,1,128,512]{2,0,1,3:T(8,128)(2,1)} %copy.62), calls=%async_computation.1 | async-start | bytes 2097152 | tf_op jit(solution)/shard_map/all_to_all | solution.py:61
  180.5 7.4 %copy.69 = bf16[32,1,4,128,128]{3,2,4,0,1:T(4,128)(2,1)} copy(bf16[32,1,4,128,128]{4,3,0,1,2:T(8,128)(2,1)} %bitcast.50) | data formatting | bytes 8388608 | tf_op jit(solution)/shard_map/reshape | solution.py:14
  188.0 7.2 %reshape.193 = bf16[32,1,512,128]{2,3,0,1:T(8,128)(2,1)} reshape(bf16[32,1,4,128,128]{3,2,4,0,1:T(4,128)(2,1)} %copy.69) | data formatting | bytes 8388608 | tf_op jit(solution)/shard_map/reshape | solution.py:14
  195.1 8.0 %fusion.19 = f32[4,128,512,8]{2,3,1,0:T(8,128)S(1)} fusion(bf16[4,8,128,512]{3,2,1,0:T(8,128)(2,1)} %bitcast.289, f32[8,8]{1,0:T(8,128)S(1)} %copy-done.8), kind=kOutput, calls=%fused_computation.22 | convolution fusion | flops 201326592 | bytes 12583168 | tf_op jit(solution)/shard_map/pt,qt...->qp.../dot_general | solution.py:28
  203.2 5.6 %fusion.64 = f32[4,8,128,512]{3,2,1,0:T(8,128)} fusion(bf16[4,8,128,512]{3,2,1,0:T(8,128)(2,1)S(1)} %bitcast.292, bf16[512,512]{1,0:T(8,128)(2,1)S(1)} %copy-done), kind=kOutput, calls=%fused_computation.78 | convolution fusion | flops 2147483648 | bytes 13107200 | tf_op jit(solution)/shard_map/dot_general | solution.py:40
  208.7 10.0 %fusion.5 = f32[4,128,512,8]{2,3,1,0:T(8,128)} fusion(f32[4,128,512,8]{2,3,1,0:T(8,128)S(1)} %fusion.19, f32[8,128,512]{2,0,1:T(8,128)S(1)} %get-tuple-element.18, f32[8,8]{1,0:T(8,128)S(1)} %copy-done.7), kind=kOutput, calls=%fused_computation.7 | convolution fusion | flops 203423744 | bytes 18874624 | tf_op jit(solution)/shard_map/ps,qp...->qs.../dot_general | solution.py:32
  218.7 20.8 %fusion.42 = bf16[4,8,128,512]{3,2,1,0:T(8,128)(2,1)} fusion(f32[4,128,512]{2,1,0:T(8,128)} %copy.73, f32[4,128,512,8]{2,3,1,0:T(8,128)} %fusion.5, f32[4,8,128,512]{3,2,1,0:T(8,128)} %fusion.64, bf16[4,8,1,128,512]{4,3,1,0,2:T(8,128)(2,1)} %bitcast.291, f32[8]{0:T(128)S(1)} %get-tuple-element.14, f32[4,8]{1,0:T(4,128)S(1)} %constant_dynamic-slice_fusion.1, ...), kind=kOutput, calls=%fused_computation.40 | convolution fusion | flops 4318035968 | bytes 31457472 | tf_op jit(solution)/shard_map/dot_general | solution.py:45
  239.5 2.8 slice_bitcast_fusion.3
  242.3 2.3 pad_maximum_fusion.1
  244.6 5.1 %all-to-all-start.3 = ((bf16[4,32,1,128,128]{4,3,1,2,0:T(8,128)(2,1)}), bf16[4,32,1,128,128]{4,3,1,2,0:T(8,128)(2,1)}, u32[]{:S(2)}, u32[]{:S(2)}) async-start(bf16[4,32,1,128,128]{4,3,1,2,0:T(8,128)(2,1)} %pad_maximum_fusion.1), calls=%async_computation.3 | async-start | bytes 8388608 | tf_op jit(solution)/shard_map/all_to_all | solution.py:13
  252.9 89.3 %all-to-all-done.3 = bf16[4,32,1,128,128]{4,3,1,2,0:T(8,128)(2,1)} async-done(((bf16[4,32,1,128,128]{4,3,1,2,0:T(8,128)(2,1)}), bf16[4,32,1,128,128]{4,3,1,2,0:T(8,128)(2,1)}, u32[]{:S(2)}, u32[]{:S(2)}) %all-to-all-start.3) | async-done | bytes 4194336 | tf_op jit(solution)/shard_map/all_to_all | solution.py:13
  342.2 4.8 %copy.74 = bf16[4,32,1,128,128]{4,3,0,1,2:T(8,128)(2,1)} copy(bf16[4,32,1,128,128]{4,3,1,2,0:T(8,128)(2,1)} %all-to-all-done.3) | data formatting | bytes 8388608 | tf_op jit(solution)/shard_map/all_to_all | solution.py:13
  347.0 6.2 %copy.75 = bf16[4,8,1,128,512]{4,3,2,1,0:T(8,128)(2,1)} copy(bf16[4,8,1,128,512]{3,4,1,0,2:T(8,128)(2,1)} %bitcast.294) | data formatting | bytes 8388608
  (34 shorter events, 15.9 us)
Async XLA Ops:
  0.6 1.1 copy-start
  0.6 4.3 %copy-start.6 = (bf16[8,1,128,512]{3,2,1,0:T(8,128)(2,1)S(1)}, bf16[8,1,128,512]{3,2,1,0:T(8,128)(2,1)}, u32[]{:S(2)}) copy-start(bf16[8,1,128,512]{3,2,1,0:T(8,128)(2,1)} %param.9) | copy-start | bytes 3145732
  1.7 6.7 %copy-start.7 = (f32[8,8]{1,0:T(8,128)S(1)}, f32[8,8]{1,0:T(8,128)}, u32[]{:S(2)}) copy-start(f32[8,8]{1,0:T(8,128)} %param.16) | copy-start | bytes 772
  4.9 6.7 %copy-start.9 = (bf16[512,512]{1,0:T(8,128)(2,1)S(1)}, bf16[512,512]{1,0:T(8,128)(2,1)}, u32[]{:S(2)}) copy-start(bf16[512,512]{1,0:T(8,128)(2,1)} %param.13) | copy-start | bytes 1572868
  5.0 6.7 %copy-start.10 = (f32[8]{0:T(128)S(1)}, f32[8]{0:T(128)}, u32[]{:S(2)}) copy-start(f32[8]{0:T(128)} %param.15) | copy-start | bytes 100
  7.1 1.3 copy-start.3
  20.5 57.2 %all-to-all-start = ((bf16[8,1,128,512]{2,0,1,3:T(8,128)(2,1)}), bf16[8,1,128,512]{2,0,1,3:T(8,128)(2,1)}, u32[]{:S(2)}, u32[]{:S(2)}) async-start(bf16[8,1,128,512]{2,0,1,3:T(8,128)(2,1)} %copy.57), calls=%async_computation | async-start | bytes 2097152 | tf_op jit(solution)/shard_map/all_to_all | solution.py:61
  27.4 3.3 copy-start.2
  30.7 5.7 %copy-start.8 = (f32[8,8]{1,0:T(8,128)S(1)}, f32[8,8]{1,0:T(8,128)}, u32[]{:S(2)}) copy-start(f32[8,8]{1,0:T(8,128)} %param.17) | copy-start | bytes 772
  77.7 98.3 %all-to-all-start.2 = ((bf16[4,32,1,128,128]{4,3,1,2,0:T(8,128)(2,1)}), bf16[4,32,1,128,128]{4,3,1,2,0:T(8,128)(2,1)}, u32[]{:S(2)}, u32[]{:S(2)}) async-start(bf16[4,32,1,128,128]{4,3,1,2,0:T(8,128)(2,1)} %pad_maximum_fusion), calls=%async_computation.2 | async-start | bytes 8388608 | tf_op jit(solution)/shard_map/all_to_all | solution.py:13
  85.5 2.1 copy-start.5
  90.4 1.3 copy-start.4
  176.0 68.6 %all-to-all-start.1 = ((bf16[8,1,128,512]{2,0,1,3:T(8,128)(2,1)}), bf16[8,1,128,512]{2,0,1,3:T(8,128)(2,1)}, u32[]{:S(2)}, u32[]{:S(2)}) async-start(bf16[8,1,128,512]{2,0,1,3:T(8,128)(2,1)} %copy.62), calls=%async_computation.1 | async-start | bytes 2097152 | tf_op jit(solution)/shard_map/all_to_all | solution.py:61
  195.1 8.0 %copy-start.1 = (bf16[32,1,512,128]{2,3,0,1:T(8,128)(2,1)S(1)}, bf16[32,1,512,128]{2,3,0,1:T(8,128)(2,1)}, u32[]{:S(2)}) copy-start(bf16[32,1,512,128]{2,3,0,1:T(8,128)(2,1)} %reshape.193) | copy-start | bytes 12582916
  244.6 97.7 %all-to-all-start.3 = ((bf16[4,32,1,128,128]{4,3,1,2,0:T(8,128)(2,1)}), bf16[4,32,1,128,128]{4,3,1,2,0:T(8,128)(2,1)}, u32[]{:S(2)}, u32[]{:S(2)}) async-start(bf16[4,32,1,128,128]{4,3,1,2,0:T(8,128)(2,1)} %pad_maximum_fusion.1), calls=%async_computation.3 | async-start | bytes 8388608 | tf_op jit(solution)/shard_map/all_to_all | solution.py:13
